TPU v7x, 256 devices: a whole 4x4x8 slice. The times are simulated.
256 devices in a mesh: dp: 8 (over y, x_lo), tensor: 32 (over z, x_hi, core).
Axes of the slice: x: 4 (x_hi: 2, x_lo: 2; x = x_hi * 2 + x_lo), y: 4, z: 8, core: 2. Of those that a mesh axis runs over, the one named last changes fastest.
Arguments:
- tokens: bfloat16 [2048, 3072], P('dp', 'tensor'), may hold values from -6 to 6
- buckets: int32 [2048], P('dp'), may hold values from 0 to 999
- modulation: float32 [1000, 3, 3072], P(None, None, 'tensor'), may hold values from -3 to 3
- up_weight: bfloat16 [3072, 12288], P(None, 'tensor'), may hold values from -0.109375 to 0.109375
- down_weight: bfloat16 [3072, 12288], P(None, 'tensor'), may hold values from -0.0546875 to 0.0546875
- output_cotangent: bfloat16 [2048, 3072], P('dp', 'tensor'), may hold values from -6 to 6
Outputs:
- mixed: bfloat16 [2048, 3072], P('dp', 'tensor')
- token_input_gradient: bfloat16 [2048, 3072], P('dp', 'tensor')
- grad_up: float32 [3072, 12288], P('dp', 'tensor')
- grad_down: float32 [3072, 12288], P('dp', 'tensor')
All inputs are finite; a program needn't handle non-finite values.
Results may differ from a plain program's by a relative error of at most 0.0062.
Values may be sent and summed in bfloat16 or wider, within the bound.
A program may use at most 64 MiB of HBM per device.

v0:
```python
import jax
import jax.numpy as jnp
from jax import lax
from jax.sharding import PartitionSpec as P


def gelu_tanh(value):
    return jax.nn.gelu(value, approximate=True)


def on_device(tokens, buckets, modulation, up_weight, down_weight, output_cotangent):
    local_cols = tokens.shape[1]
    model_width = local_cols * lax.axis_size("tensor")
    input_tokens = tokens.astype(jnp.float32)
    cond = jnp.take(modulation, buckets, axis=0)
    modulation_shift = cond[:, 0]
    modulation_scale = cond[:, 1]
    gate = cond[:, 2]
    total, squares = lax.psum(
        (jnp.sum(input_tokens, axis=1), jnp.sum(input_tokens * input_tokens, axis=1)), "tensor"
    )
    row_mean = total / model_width
    var = squares / model_width - row_mean * row_mean
    inverse_deviation = lax.rsqrt(var + 1e-06)
    normalized_input = (input_tokens - row_mean[:, None]) * inverse_deviation[:, None]
    hidden_input_rows = (normalized_input * (1.0 + modulation_scale) + modulation_shift).astype(
        jnp.bfloat16
    )
    full_in = lax.all_gather(hidden_input_rows, "tensor", axis=1, tiled=True)
    pre = jnp.dot(full_in, up_weight, preferred_element_type=jnp.float32)
    act = gelu_tanh(pre).astype(jnp.bfloat16)
    block = down_weight
    velocity = lax.psum_scatter(
        lax.dot_general(block, act, (((1,), (1,)), ((), ())), preferred_element_type=jnp.float32),
        "tensor",
        scatter_dimension=0,
        tiled=True,
    ).T
    mixed = (input_tokens + gate * velocity).astype(jnp.bfloat16)
    dvel = (output_cotangent.astype(jnp.float32) * gate).astype(jnp.bfloat16)
    full_dvel = lax.all_gather(dvel, "tensor", axis=1, tiled=True)
    dact = jnp.dot(full_dvel, down_weight, preferred_element_type=jnp.float32)
    pull = jax.vjp(gelu_tanh, pre)[1]
    dpre = pull(dact)[0].astype(jnp.bfloat16)
    block = up_weight
    dh = lax.psum_scatter(
        lax.dot_general(block, dpre, (((1,), (1,)), ((), ())), preferred_element_type=jnp.float32),
        "tensor",
        scatter_dimension=0,
        tiled=True,
    ).T
    normalized_input_gradient = dh * (1.0 + modulation_scale)
    first_product, second_product = lax.psum(
        (
            jnp.sum(normalized_input_gradient, axis=1),
            jnp.sum(normalized_input_gradient * normalized_input, axis=1),
        ),
        "tensor",
    )
    token_input_gradient = output_cotangent.astype(jnp.float32) + inverse_deviation[:, None] * (
        normalized_input_gradient
        - first_product[:, None] / model_width
        - normalized_input * second_product[:, None] / model_width
    )
    cols = full_in
    grad_up = lax.psum_scatter(
        lax.dot_general(cols, dpre, (((0,), (0,)), ((), ())), preferred_element_type=jnp.float32),
        "dp",
        scatter_dimension=0,
        tiled=True,
    )
    cols = full_dvel
    grad_down = lax.psum_scatter(
        lax.dot_general(cols, act, (((0,), (0,)), ((), ())), preferred_element_type=jnp.float32),
        "dp",
        scatter_dimension=0,
        tiled=True,
    )
    return (mixed, token_input_gradient.astype(jnp.bfloat16), grad_up, grad_down)


def solution(mesh):
    placed = (
        P("dp", "tensor"),
        P("dp"),
        P(None, None, "tensor"),
        P(None, "tensor"),
        P(None, "tensor"),
        P("dp", "tensor"),
    )
    return jax.shard_map(
        on_device,
        mesh=mesh,
        in_specs=placed,
        out_specs=(P("dp", "tensor"), P("dp", "tensor"), P("dp", "tensor"), P("dp", "tensor")),
        check_vma=False,
    )
```

profile of v0, /device:TPU:1, one launch (start us, length us, event | category | flops | bytes accessed | tf_op | source)
XLA Modules:
  0.0 722.3 jit_solution(3974144515244897455)
XLA Ops:
  7.2 0.0 copy-start
  7.2 0.0 all-gather.3.cloned.1.call-start
  7.2 0.8 compare_and_fusion
  8.1 0.7 compare_select_fusion
  8.8 0.9 copy.20
  9.7 0.1 convert_reduce_fusion
  9.8 2.8 copy.21
  12.6 2.6 gather_fusion
  15.2 0.3 broadcast_select_fusion
  15.5 0.3 fusion.23
  15.8 68.9 %all-reduce.1 = (f32[256]{0:T(256)S(1)}, f32[256]{0:T(256)S(1)}) all-reduce(f32[256]{0:T(256)S(1)} %get-tuple-element.19, f32[256]{0:T(256)S(1)} %get-tuple-element.18), channel_id=1, replica_groups=mesh['dp'=8,'tensor'=32] {'tensor'}, use_global_device_ids=true, to_apply=%region_3.4 | all-reduce | flops 512 | bytes 4096 | tf_op jit(solution)/shard_map/psum | solution.py:19
  84.7 0.1 fusion.14
  84.9 0.7 copy.24
  85.6 0.0 all-gather.3.cloned.1.call-update
  85.6 0.0 reduce-scatter.13.cloned.1.call-start
  85.7 78.6 %all-gather.3.cloned.1.call-done = bf16[256,3072]{0,1:T(8,128)(2,1)} async-done(((bf16[256,96]{0,1:T(8,128)(2,1)}), bf16[256,3072]{0,1:T(8,128)(2,1)}) %all-gather.3.cloned.1.call-update) | async-done | bytes 1572880 | tf_op jit(solution)/shard_map/all_gather | solution.py:29
  164.3 3.2 fusion.24
  167.5 0.0 copy-done
  167.5 2.7 convolution_bitcast_fusion.1
  170.2 3.5 copy.29
  173.8 0.0 copy-start.2
  173.8 0.0 reduce-scatter.13.cloned.1.call-update
  173.8 0.0 all-gather.5.cloned.1.call-start
  173.9 0.7 copy-done.2
  174.6 0.1 copy.25
  174.7 113.5 %reduce-scatter.13.cloned.1.call-done = f32[96,256]{1,0:T(8,128)} async-done(((f32[3072,256]{1,0:T(8,128)}), f32[96,256]{1,0:T(8,128)}) %reduce-scatter.13.cloned.1.call-update) | async-done | bytes 98320
  288.2 1.0 copy.30
  289.2 0.7 copy.26
  289.9 0.0 all-gather.5.cloned.1.call-update
  290.0 0.0 reduce-scatter.15.cloned.1.call-start
  290.0 84.3 %all-gather.5.cloned.1.call-done = bf16[256,3072]{0,1:T(8,128)(2,1)} async-done(((bf16[256,96]{0,1:T(8,128)(2,1)}), bf16[256,3072]{0,1:T(8,128)(2,1)}) %all-gather.5.cloned.1.call-update) | async-done | bytes 1572880 | tf_op jit(solution)/shard_map/all_gather | solution.py:41
  374.3 0.0 copy-start.1
  374.3 2.7 fusion.6
  377.1 0.0 copy-done.1
  377.1 2.7 convolution_bitcast_fusion
  379.8 3.5 copy.31
  383.3 0.0 reduce-scatter.15.cloned.1.call-update
  383.3 0.0 reduce-scatter.11.cloned.1.call-start
  383.4 4.6 fusion.22
  388.0 0.0 reduce-scatter.11.cloned.1.call-update
  388.0 0.0 reduce-scatter.9.cloned.1.call-start
  388.1 4.6 fusion.25
  392.6 0.0 reduce-scatter.9.cloned.1.call-update
  392.6 0.7 copy.27
  393.4 104.4 %reduce-scatter.15.cloned.1.call-done = f32[96,256]{1,0:T(8,128)} async-done(((f32[3072,256]{1,0:T(8,128)}), f32[96,256]{1,0:T(8,128)}) %reduce-scatter.15.cloned.1.call-update) | async-done | bytes 98320
  497.7 1.0 copy.32
  498.7 0.2 fusion.21
  499.0 72.0 %all-reduce = (f32[256]{0:T(256)S(1)}, f32[256]{0:T(256)S(1)}) all-reduce(f32[256]{0:T(256)S(1)} %get-tuple-element.17, f32[256]{0:T(256)S(1)} %get-tuple-element.16), channel_id=1, replica_groups=mesh['dp'=8,'tensor'=32] {'tensor'}, use_global_device_ids=true, to_apply=%region_9.10 | all-reduce | flops 512 | bytes 4096 | tf_op jit(solution)/shard_map/psum | solution.py:53
  571.0 0.2 fusion.8
  571.2 0.7 copy.28
  571.9 36.7 %reduce-scatter.11.cloned.1.call-done = f32[384,384]{1,0:T(8,128)} async-done(((f32[3072,384]{1,0:T(8,128)}), f32[384,384]{1,0:T(8,128)}) %reduce-scatter.11.cloned.1.call-update) | async-done | bytes 589840 | tf_op jit(solution)/shard_map/reduce_scatter | solution.py:73
  608.7 106.7 %reduce-scatter.9.cloned.1.call-done = f32[384,384]{1,0:T(8,128)} async-done(((f32[3072,384]{1,0:T(8,128)}), f32[384,384]{1,0:T(8,128)}) %reduce-scatter.9.cloned.1.call-update) | async-done | bytes 589840 | tf_op jit(solution)/shard_map/reduce_scatter | solution.py:66
  (4 shorter events, 0.1 us)
Async XLA Ops:
  7.2 160.3 %copy-start = (bf16[3072,384]{1,0:T(8,128)(2,1)S(1)}, bf16[3072,384]{1,0:T(8,128)(2,1)}, u32[]{:S(2)}) copy-start(bf16[3072,384]{1,0:T(8,128)(2,1)} %param.10) | copy-start | bytes 7077892
  7.2 157.2 %all-gather.3.cloned.1.call-start = ((), (), s32[]{:S(2)}) async-start(), calls=%async_computation.4 | async-start | bytes 1622016 | tf_op jit(solution)/shard_map/all_gather | solution.py:29
  85.6 202.5 %reduce-scatter.13.cloned.1.call-start = ((), (), s32[]{:S(2)}) async-start(), calls=%async_computation.8 | async-start | bytes 3244032
  173.8 0.8 copy-start.2
  173.8 200.5 %all-gather.5.cloned.1.call-start = ((), (), s32[]{:S(2)}) async-start(), calls=%async_computation.5 | async-start | bytes 1622016 | tf_op jit(solution)/shard_map/all_gather | solution.py:41
  290.0 207.8 %reduce-scatter.15.cloned.1.call-start = ((), (), s32[]{:S(2)}) async-start(), calls=%async_computation.9 | async-start | bytes 3244032
  374.3 2.7 copy-start.1
  383.3 225.3 %reduce-scatter.11.cloned.1.call-start = ((), (), s32[]{:S(2)}) async-start(), calls=%async_computation.7 | async-start | bytes 5308416 | tf_op jit(solution)/shard_map/reduce_scatter | solution.py:73
  388.0 327.4 %reduce-scatter.9.cloned.1.call-start = ((), (), s32[]{:S(2)}) async-start(), calls=%async_computation.6 | async-start | bytes 5308416 | tf_op jit(solution)/shard_map/reduce_scatter | solution.py:66
Sparse Core Ops, SparseCore 0:
  85.8 78.5 all-gather.2
  173.9 114.2 reduce-scatter.12
  291.6 82.7 all-gather.4
  383.5 114.2 reduce-scatter.14
  500.7 107.9 reduce-scatter.10
  611.7 103.7 reduce-scatter.8
where the time goes:
time: 723 us; the launch traced here: 722 us
  waiting for transfers between devices  524 us (72%)
  blocking collectives  141 us (20%)
  matrix products  20.5 us (3%)
  local copies, waits for them, and re-layouts  19.3 us (3%)
  between operations  14.2 us (2%)
    unnamed x8, waiting for transfers between devices  218 us
    reduce_scatter x1, waiting for transfers between devices, on_device(): lax.psum_scatter(lax.dot_general(cols, dpre, (((0,), (0,)), ((), ())), pr...  107 us
    all_gather x1, waiting for transfers between devices, on_device(): full_dvel = lax.all_gather(dvel, 'tensor', axis=1, tiled=True)  84.3 us
    all_gather x1, waiting for transfers between devices, on_device(): full_in = lax.all_gather(hidden_input_rows, 'tensor', axis=1, tiled=True)  78.6 us
    psum x1, blocking collectives, on_device(): lax.psum((jnp.sum(normalized_input_gradient, axis=1), jnp.sum(normalized_...  72 us
    psum x1, blocking collectives, on_device(): lax.psum((jnp.sum(input_tokens, axis=1), jnp.sum(input_tokens * input_tok...  68.9 us
    reduce_scatter x1, waiting for transfers between devices, on_device(): lax.psum_scatter(lax.dot_general(cols, act, (((0,), (0,)), ((), ())), pre...  36.7 us
    unnamed x15, local copies, waits for them, and re-layouts  15 us
  transfers between devices with their start and end apart: 6, of which 6 were waited for; matrix products, arithmetic and copies ran while one was open for 2% of the time, Pallas kernels for 0%

commit v1 on v0

--- a/solution.py
+++ b/solution.py
@@ -38,7 +38,9 @@
     ).T
     mixed = (input_tokens + gate * velocity).astype(jnp.bfloat16)
     dvel = (output_cotangent.astype(jnp.float32) * gate).astype(jnp.bfloat16)
-    full_dvel = lax.all_gather(dvel, "tensor", axis=1, tiled=True)
+    full_dvel = jnp.concatenate(
+        lax.all_to_all(jnp.stack([dvel] * lax.axis_size("tensor")), "tensor", 0, 0), axis=1
+    )
     dact = jnp.dot(full_dvel, down_weight, preferred_element_type=jnp.float32)
     pull = jax.vjp(gelu_tanh, pre)[1]
     dpre = pull(dact)[0].astype(jnp.bfloat16)

time: 723 us -> 690 us (0.954)
  waiting for transfers between devices: 524 us -> 442 us
  blocking collectives: 141 us -> 192 us
    all_gather x1 -> x0, waiting for transfers between devices: 84.3 us -> none  [on_device(): full_dvel = lax.all_gather(dvel, 'tensor', axis=1, tiled=True)]
    all_to_all x0 -> x1, blocking collectives: none -> 51.4 us  [on_device(): lax.all_to_all(jnp.stack([dvel] * lax.axis_size('tensor')), 'tensor', 0, 0)]
    unnamed x15 -> x17, local copies, waits for them, and re-layouts: 15 us -> 16.6 us
    unnamed x8 -> x7, waiting for transfers between devices: 218 us -> 219 us
  transfers between devices with their start and end apart: 6 -> 5, of which waited for: 6 -> 5; matrix products, arithmetic and copies ran while one was open for 2% -> 2% of each run, Pallas kernels for 0% -> 0%
where the time goes in v1:
time: 690 us
  waiting for transfers between devices  442 us (64%)
  blocking collectives  192 us (28%)
  local copies, waits for them, and re-layouts  20.5 us (3%)
  matrix products  18.9 us (3%)
  between operations  13.9 us (2%)
    unnamed x7, waiting for transfers between devices  219 us
    reduce_scatter x1, waiting for transfers between devices, on_device(): lax.psum_scatter(lax.dot_general(cols, dpre, (((0,), (0,)), ((), ())), pr...  107 us
    all_gather x1, waiting for transfers between devices, on_device(): full_in = lax.all_gather(hidden_input_rows, 'tensor', axis=1, tiled=True)  78.6 us
    psum x1, blocking collectives, on_device(): lax.psum((jnp.sum(normalized_input_gradient, axis=1), jnp.sum(normalized_...  71.7 us
    psum x1, blocking collectives, on_device(): lax.psum((jnp.sum(input_tokens, axis=1), jnp.sum(input_tokens * input_tok...  68.9 us
    all_to_all x1, blocking collectives, on_device(): lax.all_to_all(jnp.stack([dvel] * lax.axis_size('tensor')), 'tensor', 0, 0)  51.4 us
    reduce_scatter x1, waiting for transfers between devices, on_device(): lax.psum_scatter(lax.dot_general(cols, act, (((0,), (0,)), ((), ())), pre...  36.6 us
    unnamed x17, local copies, waits for them, and re-layouts  16.6 us
  transfers between devices with their start and end apart: 5, of which 5 were waited for; matrix products, arithmetic and copies ran while one was open for 2% of the time, Pallas kernels for 0%

profile of v1, /device:TPU:1, one launch (start us, length us, event | category | flops | bytes accessed | tf_op | source)
XLA Modules:
  0.0 689.6 jit_solution(454933059821965631)
XLA Ops:
  7.2 0.0 copy-start
  7.2 0.0 all-gather.2.cloned.1.call-start
  7.2 0.8 compare_and_fusion
  8.1 0.7 compare_select_fusion
  8.8 0.9 copy.21
  9.7 0.1 convert_reduce_fusion
  9.8 2.8 copy.22
  12.6 2.6 gather_fusion
  15.2 0.3 broadcast_select_fusion
  15.5 0.3 fusion.23
  15.8 68.9 %all-reduce.1 = (f32[256]{0:T(256)S(1)}, f32[256]{0:T(256)S(1)}) all-reduce(f32[256]{0:T(256)S(1)} %get-tuple-element.19, f32[256]{0:T(256)S(1)} %get-tuple-element.18), channel_id=1, replica_groups=mesh['dp'=8,'tensor'=32] {'tensor'}, use_global_device_ids=true, to_apply=%region_3.4 | all-reduce | flops 512 | bytes 4096 | tf_op jit(solution)/shard_map/psum | solution.py:19
  84.7 0.1 fusion.14
  84.9 0.7 copy.25
  85.6 0.0 all-gather.2.cloned.1.call-update
  85.6 0.0 reduce-scatter.13.cloned.1.call-start
  85.7 78.6 %all-gather.2.cloned.1.call-done = bf16[256,3072]{0,1:T(8,128)(2,1)} async-done(((bf16[256,96]{0,1:T(8,128)(2,1)}), bf16[256,3072]{0,1:T(8,128)(2,1)}) %all-gather.2.cloned.1.call-update) | async-done | bytes 1572880 | tf_op jit(solution)/shard_map/all_gather | solution.py:29
  164.3 3.2 fusion.24
  167.5 0.0 copy-done
  167.5 2.7 convolution_bitcast_fusion.1
  170.2 3.5 copy.30
  173.8 0.0 copy-start.3
  173.8 0.0 reduce-scatter.13.cloned.1.call-update
  173.8 0.0 reduce-scatter.15.cloned.1.call-start
  173.9 0.7 copy-done.3
  174.6 0.1 copy.26
  174.7 113.5 %reduce-scatter.13.cloned.1.call-done = f32[96,256]{1,0:T(8,128)} async-done(((f32[3072,256]{1,0:T(8,128)}), f32[96,256]{1,0:T(8,128)}) %reduce-scatter.13.cloned.1.call-update) | async-done | bytes 98320
  288.2 1.0 copy.31
  289.2 0.1 copy.27
  289.3 0.2 stack.2
  289.5 51.4 %all_to_all.5 = bf16[32,256,96]{1,2,0:T(8,128)(2,1)S(1)} all-to-all(bf16[32,256,96]{1,2,0:T(8,128)(2,1)S(1)} %stack.2), channel_id=1, replica_groups=mesh['dp'=8,'tensor'=32] {'tensor'}, dimensions={0} | all-to-all | bytes 3145728 | tf_op jit(solution)/shard_map/all_to_all | solution.py:42
  340.9 0.0 copy-start.1
  340.9 1.2 copy-done.1
  342.0 0.0 copy-start.2
  342.0 1.2 fusion.6
  343.2 0.5 copy-done.2
  343.7 2.7 convolution_bitcast_fusion
  346.4 3.5 copy.32
  349.9 0.0 reduce-scatter.15.cloned.1.call-update
  349.9 0.0 reduce-scatter.11.cloned.1.call-start
  350.0 4.6 fusion.22
  354.6 0.0 reduce-scatter.11.cloned.1.call-update
  354.6 0.0 reduce-scatter.9.cloned.1.call-start
  354.7 4.6 fusion.25
  359.2 0.0 reduce-scatter.9.cloned.1.call-update
  359.3 0.7 copy.28
  360.0 105.9 %reduce-scatter.15.cloned.1.call-done = f32[96,256]{1,0:T(8,128)} async-done(((f32[3072,256]{1,0:T(8,128)}), f32[96,256]{1,0:T(8,128)}) %reduce-scatter.15.cloned.1.call-update) | async-done | bytes 98320
  465.9 1.0 copy.33
  466.9 0.2 fusion.21
  467.1 71.7 %all-reduce = (f32[256]{0:T(256)S(1)}, f32[256]{0:T(256)S(1)}) all-reduce(f32[256]{0:T(256)S(1)} %get-tuple-element.17, f32[256]{0:T(256)S(1)} %get-tuple-element.16), channel_id=1, replica_groups=mesh['dp'=8,'tensor'=32] {'tensor'}, use_global_device_ids=true, to_apply=%region_9.10 | all-reduce | flops 512 | bytes 4096 | tf_op jit(solution)/shard_map/psum | solution.py:55
  538.8 0.2 fusion.8
  539.0 0.7 copy.29
  539.7 36.6 %reduce-scatter.11.cloned.1.call-done = f32[384,384]{1,0:T(8,128)} async-done(((f32[3072,384]{1,0:T(8,128)}), f32[384,384]{1,0:T(8,128)}) %reduce-scatter.11.cloned.1.call-update) | async-done | bytes 589840 | tf_op jit(solution)/shard_map/reduce_scatter | solution.py:75
  576.4 106.7 %reduce-scatter.9.cloned.1.call-done = f32[384,384]{1,0:T(8,128)} async-done(((f32[3072,384]{1,0:T(8,128)}), f32[384,384]{1,0:T(8,128)}) %reduce-scatter.9.cloned.1.call-update) | async-done | bytes 589840 | tf_op jit(solution)/shard_map/reduce_scatter | solution.py:68
  (4 shorter events, 0.1 us)
Async XLA Ops:
  7.2 160.3 %copy-start = (bf16[3072,384]{1,0:T(8,128)(2,1)S(1)}, bf16[3072,384]{1,0:T(8,128)(2,1)}, u32[]{:S(2)}) copy-start(bf16[3072,384]{1,0:T(8,128)(2,1)} %param.10) | copy-start | bytes 7077892
  7.2 157.2 %all-gather.2.cloned.1.call-start = ((), (), s32[]{:S(2)}) async-start(), calls=%async_computation.5 | async-start | bytes 1622016 | tf_op jit(solution)/shard_map/all_gather | solution.py:29
  85.6 202.5 %reduce-scatter.13.cloned.1.call-start = ((), (), s32[]{:S(2)}) async-start(), calls=%async_computation.8 | async-start | bytes 3244032
  173.8 0.8 copy-start.3
  173.8 292.1 %reduce-scatter.15.cloned.1.call-start = ((), (), s32[]{:S(2)}) async-start(), calls=%async_computation.9 | async-start | bytes 3244032
  340.9 1.2 copy-start.1
  342.0 1.7 copy-start.2
  349.9 226.4 %reduce-scatter.11.cloned.1.call-start = ((), (), s32[]{:S(2)}) async-start(), calls=%async_computation.7 | async-start | bytes 5308416 | tf_op jit(solution)/shard_map/reduce_scatter | solution.py:75
  354.6 328.5 %reduce-scatter.9.cloned.1.call-start = ((), (), s32[]{:S(2)}) async-start(), calls=%async_computation.6 | async-start | bytes 5308416 | tf_op jit(solution)/shard_map/reduce_scatter | solution.py:68
Sparse Core Ops, SparseCore 0:
  85.8 78.5 all-gather.1
  173.9 114.2 reduce-scatter.12
  350.1 115.8 reduce-scatter.14
  468.9 107.4 reduce-scatter.10
  579.4 103.7 reduce-scatter.8
